TPU v7x, 32 devices: a whole 2x2x4 slice. The times are simulated.
32 devices in a mesh: groups: 2 (over y), blk: 4 (over z), uly: 2 (over x), cfg: 2 (over core).
Axes of the slice: x: 2, y: 2, z: 4, core: 2. Of those that a mesh axis runs over, the one named last changes fastest.
Arguments:
- query_rows: bfloat16 [2, 1024, 1536], P('cfg', ('groups', 'blk', 'uly')), parts along dimension 1, may hold values from -6 to 6
- key_rows: bfloat16 [2, 1024, 1536], P('cfg', ('groups', 'blk', 'uly')), parts along dimension 1, may hold values from -6 to 6
- value_rows: bfloat16 [2, 1024, 1536], P('cfg', ('groups', 'blk', 'uly')), parts along dimension 1, may hold values from -6 to 6
Outputs:
- attended: bfloat16 [2, 1024, 1536], P('cfg', ('groups', 'blk', 'uly')), parts along dimension 1
There are 2 independent parts, one for each index of `groups`. A program takes and returns all parts, laid end to end along the dimension named above; each array names one. Nothing has to cross between parts.
All inputs are finite; a program needn't handle non-finite values.
Results may differ from a plain program's by a relative error of at most 0.0045.
Values may be sent and summed in bfloat16 or wider, within the bound.
A program may use at most 128 MiB of HBM per device.

v0:
```python
import math

import jax
import jax.numpy as jnp
from jax import lax
from jax.sharding import PartitionSpec as P

HD = 128


def attend(queries, key_part, value_part):
    query_mat = queries[0, :, 0]
    row_count, head_count, head_size = query_mat.shape
    score_scale = 1.0 / math.sqrt(head_size)
    start_state = (
        jnp.full((head_count, row_count), -1e30, jnp.float32),
        jnp.zeros((head_count, row_count), jnp.float32),
        jnp.zeros((row_count, head_count, head_size), jnp.float32),
    )

    def absorb(state, pieces):
        key_piece = pieces[0][0, :, 0]
        value_piece = pieces[1][0, :, 0]
        scores = (
            jnp.einsum("qhd,khd->hqk", query_mat, key_piece, preferred_element_type=jnp.float32)
            * score_scale
        )
        running, totals, accumulated = state
        new_max = jnp.maximum(running, jnp.max(scores, axis=2))
        weights = jnp.exp(scores - new_max[:, :, None])
        factor = jnp.exp(running - new_max)
        totals = totals * factor + jnp.sum(weights, axis=2)
        probabilities = weights.astype(jnp.bfloat16)
        contrib = jnp.einsum(
            "hqk,khd->qhd", probabilities, value_piece, preferred_element_type=jnp.float32
        )
        accumulated = accumulated * factor.T[:, :, None] + contrib
        return (new_max, totals, accumulated)

    whole_keys, whole_values = (
        lax.all_gather(key_part, "blk", axis=1, tiled=True),
        lax.all_gather(value_part, "blk", axis=1, tiled=True),
    )
    key_count = whole_keys.shape[1]
    block_rows = math.gcd(key_count, 1024)

    def one_block(state, counter):
        offset = counter * block_rows
        key_block = lax.dynamic_slice_in_dim(whole_keys, offset, block_rows, 1)
        value_block = lax.dynamic_slice_in_dim(whole_values, offset, block_rows, 1)
        return (absorb(state, (key_block, value_block)), None)

    result, unused = lax.scan(
        one_block, start_state, jnp.arange(key_count // block_rows, dtype=jnp.int32)
    )
    output = (result[2] / result[1].T[:, :, None]).astype(jnp.bfloat16)
    return output.reshape(1, row_count, 1, head_count, head_size)


def regroup_back(attended_part):
    return lax.all_to_all(attended_part, "uly", split_axis=1, concat_axis=2, tiled=True)


def whole_pass(triple):
    return regroup_back(attend(triple[0], triple[1], triple[2]))


def local(query_rows, key_rows, value_rows):
    ulysses = lax.axis_size("uly")
    tokens = query_rows.shape[1]
    width = query_rows.shape[2]
    heads_local = width // HD // ulysses

    def split_heads(array):
        return array.reshape(1, tokens, ulysses, heads_local, HD)

    sectioned = (split_heads(query_rows), split_heads(key_rows), split_heads(value_rows))
    moved = (
        lax.all_to_all(sectioned[0], "uly", split_axis=2, concat_axis=1, tiled=True),
        lax.all_to_all(sectioned[1], "uly", split_axis=2, concat_axis=1, tiled=True),
        lax.all_to_all(sectioned[2], "uly", split_axis=2, concat_axis=1, tiled=True),
    )
    merged = whole_pass(moved)
    return merged.reshape(1, tokens, width)


def solution(mesh):
    in_specs = (
        P("cfg", ("groups", "blk", "uly"), None),
        P("cfg", ("groups", "blk", "uly"), None),
        P("cfg", ("groups", "blk", "uly"), None),
    )
    out_specs = P("cfg", ("groups", "blk", "uly"), None)
    return jax.shard_map(local, mesh=mesh, in_specs=in_specs, out_specs=out_specs, check_vma=False)
```

profile of v0, /device:TPU:0, one launch (start us, length us, event | category | flops | bytes accessed | tf_op | source)
XLA Modules:
  0.0 69.2 jit_solution(18183577460159070147)
XLA Ops:
  0.0 0.0 copy-start
  0.0 1.2 %reshape.23 = bf16[1,64,2,6,128]{4,3,2,1,0:T(8,128)(2,1)S(1)} reshape(bf16[1,64,1536]{2,1,0:T(8,128)(2,1)} %param.4) | data formatting | bytes 393216 | tf_op jit(solution)/shard_map/reshape | solution.py:75
  1.2 0.7 %copy.14 = bf16[1,64,2,6,128]{4,1,3,0,2:T(8,128)(2,1)} copy(bf16[1,64,2,6,128]{4,3,2,1,0:T(8,128)(2,1)S(1)} %reshape.23) | data formatting | bytes 393216 | tf_op jit(solution)/shard_map/reshape | solution.py:75
  1.9 4.2 %all-to-all-start.1 = ((bf16[1,64,2,6,128]{4,1,3,0,2:T(8,128)(2,1)}), bf16[1,64,2,6,128]{4,1,3,0,2:T(8,128)(2,1)S(1)}, u32[]{:S(2)}, u32[]{:S(2)}) async-start(bf16[1,64,2,6,128]{4,1,3,0,2:T(8,128)(2,1)} %copy.14), calls=%async_computation.1 | async-start | bytes 393216 | tf_op jit(solution)/shard_map/all_to_all | solution.py:80
  6.2 1.2 %reshape.22 = bf16[1,64,2,6,128]{4,3,2,1,0:T(8,128)(2,1)S(1)} reshape(bf16[1,64,1536]{2,1,0:T(8,128)(2,1)} %param.3) | data formatting | bytes 393216 | tf_op jit(solution)/shard_map/reshape | solution.py:75
  7.3 0.7 %copy.12 = bf16[1,64,2,6,128]{4,1,3,0,2:T(8,128)(2,1)} copy(bf16[1,64,2,6,128]{4,3,2,1,0:T(8,128)(2,1)S(1)} %reshape.22) | data formatting | bytes 393216 | tf_op jit(solution)/shard_map/reshape | solution.py:75
  8.1 0.0 copy-done
  8.1 0.2 reshape.24
  8.3 0.7 %copy.16 = bf16[1,64,2,6,128]{4,1,3,0,2:T(8,128)(2,1)} copy(bf16[1,64,2,6,128]{4,3,2,1,0:T(8,128)(2,1)S(1)} %reshape.24) | data formatting | bytes 393216 | tf_op jit(solution)/shard_map/reshape | solution.py:75
  9.0 2.3 %all-to-all-done.1 = bf16[1,64,2,6,128]{4,1,3,0,2:T(8,128)(2,1)S(1)} async-done(((bf16[1,64,2,6,128]{4,1,3,0,2:T(8,128)(2,1)}), bf16[1,64,2,6,128]{4,1,3,0,2:T(8,128)(2,1)S(1)}, u32[]{:S(2)}, u32[]{:S(2)}) %all-to-all-start.1) | async-done | bytes 196640 | tf_op jit(solution)/shard_map/all_to_all | solution.py:80
  11.3 3.4 %all-to-all-start = ((bf16[1,64,2,6,128]{4,1,3,0,2:T(8,128)(2,1)}), bf16[1,64,2,6,128]{4,1,3,0,2:T(8,128)(2,1)S(1)}, u32[]{:S(2)}, u32[]{:S(2)}) async-start(bf16[1,64,2,6,128]{4,1,3,0,2:T(8,128)(2,1)} %copy.12), calls=%async_computation | async-start | bytes 393216 | tf_op jit(solution)/shard_map/all_to_all | solution.py:79
  14.8 20.0 %all_gather.6 = bf16[1,512,1,6,128]{4,1,3,2,0:T(8,128)(2,1)S(1)} all-gather(bf16[1,128,1,6,128]{4,1,3,2,0:T(8,128)(2,1)S(1)} %bitcast.51), channel_id=1, replica_groups=mesh['groups'=2,'blk'=4,'uly'=2,'cfg'=2] {'blk'}, dimensions={1}, use_global_device_ids=true | all-gather | bytes 983040 | tf_op jit(solution)/shard_map/all_gather | solution.py:41
  34.8 0.0 all-to-all-done
  34.8 3.4 %all-to-all-start.2 = ((bf16[1,64,2,6,128]{4,1,3,0,2:T(8,128)(2,1)}), bf16[1,64,2,6,128]{4,1,3,0,2:T(8,128)(2,1)S(1)}, u32[]{:S(2)}, u32[]{:S(2)}) async-start(bf16[1,64,2,6,128]{4,1,3,0,2:T(8,128)(2,1)} %copy.16), calls=%async_computation.2 | async-start | bytes 393216 | tf_op jit(solution)/shard_map/all_to_all | solution.py:81
  38.2 0.4 fusion.10
  38.7 0.5 fusion
  39.2 3.8 %all-to-all-done.2 = bf16[1,64,2,6,128]{4,1,3,0,2:T(8,128)(2,1)S(1)} async-done(((bf16[1,64,2,6,128]{4,1,3,0,2:T(8,128)(2,1)}), bf16[1,64,2,6,128]{4,1,3,0,2:T(8,128)(2,1)S(1)}, u32[]{:S(2)}, u32[]{:S(2)}) %all-to-all-start.2) | async-done | bytes 196640 | tf_op jit(solution)/shard_map/all_to_all | solution.py:81
  43.0 17.0 %all_gather.7 = bf16[1,512,1,6,128]{4,1,3,2,0:T(8,128)(2,1)S(1)} all-gather(bf16[1,128,1,6,128]{4,1,3,2,0:T(8,128)(2,1)S(1)} %bitcast.52), channel_id=1, replica_groups=mesh['groups'=2,'blk'=4,'uly'=2,'cfg'=2] {'blk'}, dimensions={1}, use_global_device_ids=true | all-gather | bytes 983040 | tf_op jit(solution)/shard_map/all_gather | solution.py:42
  60.0 0.5 fusion.5
  60.6 0.1 copy.18
  60.7 7.6 %all_to_all.66 = bf16[1,128,1,6,128]{4,3,2,0,1:T(8,128)(2,1)S(1)} all-to-all(bf16[1,128,1,6,128]{4,3,2,0,1:T(8,128)(2,1)S(1)} %copy.18), channel_id=1, replica_groups=mesh['groups'=2,'blk'=4,'uly'=2,'cfg'=2] {'uly'}, dimensions={1} | all-to-all | bytes 393216 | tf_op jit(solution)/shard_map/all_to_all | solution.py:61
  68.3 0.9 %reshape.26 = bf16[1,64,1536]{2,1,0:T(8,128)(2,1)} reshape(bf16[1,64,2,1,6,128]{5,4,2,1,3,0:T(8,128)(2,1)S(1)} %bitcast.45) | data formatting | bytes 393216 | tf_op jit(solution)/shard_map/reshape | solution.py:84
  (6 shorter events, 0.1 us)
Async XLA Ops:
  0.0 8.1 %copy-start = (bf16[1,64,1536]{2,1,0:T(8,128)(2,1)S(1)}, bf16[1,64,1536]{2,1,0:T(8,128)(2,1)}, u32[]{:S(2)}) copy-start(bf16[1,64,1536]{2,1,0:T(8,128)(2,1)} %param.5) | copy-start | bytes 589828
  1.9 9.4 %all-to-all-start.1 = ((bf16[1,64,2,6,128]{4,1,3,0,2:T(8,128)(2,1)}), bf16[1,64,2,6,128]{4,1,3,0,2:T(8,128)(2,1)S(1)}, u32[]{:S(2)}, u32[]{:S(2)}) async-start(bf16[1,64,2,6,128]{4,1,3,0,2:T(8,128)(2,1)} %copy.14), calls=%async_computation.1 | async-start | bytes 393216 | tf_op jit(solution)/shard_map/all_to_all | solution.py:80
  11.3 23.5 %all-to-all-start = ((bf16[1,64,2,6,128]{4,1,3,0,2:T(8,128)(2,1)}), bf16[1,64,2,6,128]{4,1,3,0,2:T(8,128)(2,1)S(1)}, u32[]{:S(2)}, u32[]{:S(2)}) async-start(bf16[1,64,2,6,128]{4,1,3,0,2:T(8,128)(2,1)} %copy.12), calls=%async_computation | async-start | bytes 393216 | tf_op jit(solution)/shard_map/all_to_all | solution.py:79
  34.8 8.2 %all-to-all-start.2 = ((bf16[1,64,2,6,128]{4,1,3,0,2:T(8,128)(2,1)}), bf16[1,64,2,6,128]{4,1,3,0,2:T(8,128)(2,1)S(1)}, u32[]{:S(2)}, u32[]{:S(2)}) async-start(bf16[1,64,2,6,128]{4,1,3,0,2:T(8,128)(2,1)} %copy.16), calls=%async_computation.2 | async-start | bytes 393216 | tf_op jit(solution)/shard_map/all_to_all | solution.py:81
where the time goes:
time: 69.6 us; the launch traced here: 69.2 us
  blocking collectives  44.5 us (64%)
  starting transfers between devices  11.1 us (16%)
  waiting for transfers between devices  6.09 us (9%)
  local copies, waits for them, and re-layouts  5.94 us (9%)
  matrix products  0.98 us (1%)
    all_gather x1, blocking collectives, attend(): lax.all_gather(key_part, 'blk', axis=1, tiled=True)  20 us
    all_gather x1, blocking collectives, attend(): lax.all_gather(value_part, 'blk', axis=1, tiled=True)  17 us
    all_to_all x1, blocking collectives, regroup_back(): lax.all_to_all(attended_part, 'uly', split_axis=1, concat_axis=2, tiled=T...  7.56 us
    reshape x6, local copies, waits for them, and re-layouts, split_heads(): return array.reshape(1, tokens, ulysses, heads_local, HD)  4.8 us
    all_to_all x1, starting transfers between devices, local(): lax.all_to_all(sectioned[1], 'uly', split_axis=2, concat_axis=1, tiled=True)  4.23 us
    all_to_all x1, waiting for transfers between devices, local(): lax.all_to_all(sectioned[2], 'uly', split_axis=2, concat_axis=1, tiled=True)  3.81 us
    all_to_all x1, starting transfers between devices, local(): lax.all_to_all(sectioned[0], 'uly', split_axis=2, concat_axis=1, tiled=True)  3.43 us
    all_to_all x1, starting transfers between devices, local(): lax.all_to_all(sectioned[2], 'uly', split_axis=2, concat_axis=1, tiled=True)  3.43 us
  transfers between devices with their start and end apart: 3, of which 2 were waited for; matrix products, arithmetic and copies ran while one was open for 6% of the time, Pallas kernels for 0%

commit v1 on v0

--- a/solution.py
+++ b/solution.py
@@ -1,11 +1,15 @@
+import functools
 import math
 
 import jax
 import jax.numpy as jnp
 from jax import lax
+from jax.experimental import pallas as pl
+from jax.experimental.pallas import tpu as pltpu
 from jax.sharding import PartitionSpec as P
 
 HD = 128
+MESH = pl.DeviceIdType.MESH
 
 
 def attend(queries, key_part, value_part):
@@ -57,38 +61,240 @@
     return output.reshape(1, row_count, 1, head_count, head_size)
 
 
-def regroup_back(attended_part):
-    return lax.all_to_all(attended_part, "uly", split_axis=1, concat_axis=2, tiled=True)
-
-
-def whole_pass(triple):
-    return regroup_back(attend(triple[0], triple[1], triple[2]))
-
-
-def local(query_rows, key_rows, value_rows):
+def gathered(query_rows, key_rows, value_rows):
     ulysses = lax.axis_size("uly")
     tokens = query_rows.shape[1]
     width = query_rows.shape[2]
     heads_local = width // HD // ulysses
 
-    def split_heads(array):
-        return array.reshape(1, tokens, ulysses, heads_local, HD)
-
-    sectioned = (split_heads(query_rows), split_heads(key_rows), split_heads(value_rows))
-    moved = (
-        lax.all_to_all(sectioned[0], "uly", split_axis=2, concat_axis=1, tiled=True),
-        lax.all_to_all(sectioned[1], "uly", split_axis=2, concat_axis=1, tiled=True),
-        lax.all_to_all(sectioned[2], "uly", split_axis=2, concat_axis=1, tiled=True),
+    def moved(array):
+        sections = array.reshape(1, tokens, ulysses, heads_local, HD)
+        return lax.all_to_all(sections, "uly", split_axis=2, concat_axis=1, tiled=True)
+
+    mixed = attend(moved(query_rows), moved(key_rows), moved(value_rows))
+    merged = lax.all_to_all(mixed, "uly", split_axis=1, concat_axis=2, tiled=True)
+    return merged.reshape(1, tokens, width)
+
+
+def head_counts(heads_column, blocks):
+    counts = [heads_column // blocks] * blocks
+    by_middle = sorted(range(blocks), key=lambda z: (abs(2 * z - (blocks - 1)), z))
+    for z in by_middle[: heads_column % blocks]:
+        counts[z] += 1
+    return counts
+
+
+def exchange_kernel(
+    blocks, ulys, rows, heads, q_ref, k_ref, v_ref, o_ref,
+    qb, kb, vb, pb, ob, in_send, in_recv, out_send, out_recv,
+):
+    peers = blocks * ulys
+    column = heads // ulys
+    counts = head_counts(column, blocks)
+    starts = [sum(counts[:z]) for z in range(blocks)]
+    slots = max(counts)
+    z = lax.axis_index("blk")
+    x = lax.axis_index("uly")
+    me = z * ulys + x
+    sources = (q_ref, k_ref, v_ref)
+    buffers = (qb, kb, vb)
+    fold = (1.0 / math.sqrt(HD)) * math.log2(math.e)
+    chunk_rows = ulys * rows
+
+    def head_of(pz, px, s):
+        return px * column + starts[pz] + s
+
+    def owned(pz, px):
+        return [head_of(pz, px, s) for s in range(counts[pz])]
+
+    def piece(t, head):
+        return sources[t].at[0, :, pl.ds(head * HD, HD)]
+
+    def send_order(mz, mx):
+        half = blocks // 2
+        def rank(p):
+            pz, px = p // ulys, p % ulys
+            crosses = (pz < half) != (mz < half)
+            return (not crosses, -abs(pz - mz), px == mx)
+        return sorted((p for p in range(peers) if p != mz * ulys + mx), key=rank)
+
+    def copies(mp):
+        mz, mx = mp // ulys, mp % ulys
+        made = []
+        for s in range(slots):
+            for group in ((0, 1), (2,)):
+                for p in send_order(mz, mx):
+                    pz, px = p // ulys, p % ulys
+                    if s >= counts[pz]:
+                        continue
+                    for t in group:
+                        made.append(
+                            pltpu.make_async_remote_copy(
+                                src_ref=piece(t, head_of(pz, px, s)),
+                                dst_ref=buffers[t].at[s, pl.ds(mp * rows, rows)],
+                                send_sem=in_send.at[s, t, p],
+                                recv_sem=in_recv.at[s, t, mp],
+                                device_id={"blk": pz, "uly": px},
+                                device_id_type=MESH,
+                            )
+                        )
+        return made
+
+    barrier = pltpu.get_barrier_semaphore()
+    for d in range(1, peers):
+        peer = lax.rem(me + d, peers)
+        pl.semaphore_signal(
+            barrier, inc=1,
+            device_id={"blk": peer // ulys, "uly": lax.rem(peer, ulys)},
+            device_id_type=MESH,
+        )
+    for mp in range(peers):
+        @pl.when(me == mp)
+        def _():
+            for s, head in enumerate(owned(mp // ulys, mp % ulys)):
+                for t in range(3):
+                    pltpu.make_async_copy(
+                        piece(t, head), buffers[t].at[s, pl.ds(mp * rows, rows)],
+                        in_recv.at[s, t, mp],
+                    ).start()
+    pl.semaphore_wait(barrier, peers - 1)
+
+    for mp in range(peers):
+        @pl.when(me == mp)
+        def _():
+            for copy in copies(mp):
+                copy.start()
+
+    first = jnp.int32(0)
+    for i in range(blocks):
+        first = first + jnp.where(z > i, counts[i], 0)
+    my_head = x * column + first
+    turn = jnp.where(z < blocks // 2, blocks // 2, 0)
+
+    def landed(s, t):
+        for p in range(peers):
+            block = buffers[t].at[s, pl.ds(p * rows, rows)]
+            pltpu.make_async_copy(block, block, in_recv.at[s, t, p]).wait()
+
+    def out_copy(s, c, px):
+        head = pl.multiple_of((my_head + s) * HD, HD)
+        begin = pl.multiple_of((c * ulys + px) * rows, rows)
+        return ob.at[s, pl.ds(begin, rows)], o_ref.at[0, :, pl.ds(head, HD)]
+
+    def out_remote(s, c, px):
+        src, dst = out_copy(s, c, px)
+        return pltpu.make_async_remote_copy(
+            src_ref=src, dst_ref=dst,
+            send_sem=out_send.at[s, c * ulys + px],
+            recv_sem=out_recv.at[my_head + s],
+            device_id={"blk": c, "uly": px}, device_id_type=MESH,
+        )
+
+    def out_local(s, c, px):
+        src, dst = out_copy(s, c, px)
+        return pltpu.make_async_copy(src, dst, out_recv.at[my_head + s])
+
+    def one_slot(s):
+        landed(s, 0)
+        landed(s, 1)
+        totals = []
+        for i in range(blocks):
+            c = lax.rem(turn + i, blocks)
+            span = pl.ds(pl.multiple_of(c * chunk_rows, chunk_rows), chunk_rows)
+            scores = lax.dot_general(
+                qb[s, span, :], kb[s], (((1,), (1,)), ((), ())),
+                preferred_element_type=jnp.float32,
+            )
+            top = jnp.max(scores, axis=1, keepdims=True)
+            weights = jnp.exp2((scores - top) * fold)
+            totals.append(jnp.sum(weights, axis=1, keepdims=True))
+            pb[span, :] = weights.astype(jnp.bfloat16)
+        landed(s, 2)
+        for i in range(blocks):
+            c = lax.rem(turn + i, blocks)
+            span = pl.ds(pl.multiple_of(c * chunk_rows, chunk_rows), chunk_rows)
+            mixed = jnp.dot(pb[span, :], vb[s], preferred_element_type=jnp.float32)
+            ob[s, span, :] = (mixed / totals[i]).astype(jnp.bfloat16)
+            for px in range(ulys):
+                mine = jnp.logical_and(c == z, x == px)
+
+                @pl.when(mine)
+                def _():
+                    out_local(s, c, px).start()
+
+                @pl.when(jnp.logical_not(mine))
+                def _():
+                    out_remote(s, c, px).start()
+
+    def holds(s):
+        has = z < 0
+        for i in range(blocks):
+            if counts[i] > s:
+                has = jnp.logical_or(has, z == i)
+        return has
+
+    for s in range(slots):
+        if min(counts) > s:
+            one_slot(s)
+        else:
+            pl.when(holds(s))(functools.partial(one_slot, s))
+
+    for head in range(heads):
+        block = o_ref.at[0, :, pl.ds(head * HD, HD)]
+        pltpu.make_async_copy(block, block, out_recv.at[head]).wait()
+
+    for mp in range(peers):
+        @pl.when(me == mp)
+        def _():
+            mz, mx = mp // ulys, mp % ulys
+            for copy in copies(mp):
+                copy.wait_send()
+            for s in range(counts[mz]):
+                for p in range(peers):
+                    if p != mp:
+                        out_remote(s, p // ulys, p % ulys).wait_send()
+
+
+def exchanged(query_rows, key_rows, value_rows):
+    blocks = lax.axis_size("blk")
+    ulys = lax.axis_size("uly")
+    unused, rows, width = query_rows.shape
+    heads = width // HD
+    peers = blocks * ulys
+    slots = max(head_counts(heads // ulys, blocks))
+    total = peers * rows
+    return pl.pallas_call(
+        functools.partial(exchange_kernel, blocks, ulys, rows, heads),
+        out_shape=jax.ShapeDtypeStruct(query_rows.shape, jnp.bfloat16),
+        in_specs=[pl.BlockSpec(memory_space=pl.ANY)] * 3,
+        out_specs=pl.BlockSpec(memory_space=pl.ANY),
+        scratch_shapes=[
+            pltpu.VMEM((slots, total, HD), jnp.bfloat16),
+            pltpu.VMEM((slots, total, HD), jnp.bfloat16),
+            pltpu.VMEM((slots, total, HD), jnp.bfloat16),
+            pltpu.VMEM((total, total), jnp.bfloat16),
+            pltpu.VMEM((slots, total, HD), jnp.bfloat16),
+            pltpu.SemaphoreType.DMA((slots, 3, peers)),
+            pltpu.SemaphoreType.DMA((slots, 3, peers)),
+            pltpu.SemaphoreType.DMA((slots, peers)),
+            pltpu.SemaphoreType.DMA((heads,)),
+        ],
+        compiler_params=pltpu.CompilerParams(collective_id=0, has_side_effects=True),
+    )(query_rows, key_rows, value_rows)
+
+
+def local(query_rows, key_rows, value_rows):
+    blocks = lax.axis_size("blk")
+    ulys = lax.axis_size("uly")
+    heads = query_rows.shape[2] // HD
+    tokens = query_rows.shape[1] * blocks * ulys
+    if heads % ulys == 0 and heads // ulys >= blocks and tokens <= 1024:
+        return exchanged(query_rows, key_rows, value_rows)
+    return gathered(query_rows, key_rows, value_rows)
+
+
+def solution(mesh):
+    spec = P("cfg", ("groups", "blk", "uly"), None)
+    return jax.shard_map(
+        local, mesh=mesh, in_specs=(spec, spec, spec), out_specs=spec, check_vma=False
     )
-    merged = whole_pass(moved)
-    return merged.reshape(1, tokens, width)
-
-
-def solution(mesh):
-    in_specs = (
-        P("cfg", ("groups", "blk", "uly"), None),
-        P("cfg", ("groups", "blk", "uly"), None),
-        P("cfg", ("groups", "blk", "uly"), None),
-    )
-    out_specs = P("cfg", ("groups", "blk", "uly"), None)
-    return jax.shard_map(local, mesh=mesh, in_specs=in_specs, out_specs=out_specs, check_vma=False)

time: 69.6 us -> 29.2 us (0.42)
  blocking collectives: 44.5 us -> 0 us
  Pallas kernels: 0 us -> 27.5 us
  starting transfers between devices: 11.1 us -> 0 us
  waiting for transfers between devices: 6.09 us -> 0 us
  local copies, waits for them, and re-layouts: 5.94 us -> 1.62 us
  matrix products: 0.98 us -> 0 us
    all_gather x2 -> x0, blocking collectives: 37 us -> none  [the longest x1 20 us: attend(): lax.all_gather(key_part, 'blk', axis=1, tiled=True)]
    pallas_call x0 -> x1, Pallas kernels: none -> 27.5 us  [exchanged(): pl.pallas_call(functools.partial(exchange_kernel, blocks, ulys, rows, hea...]
    all_to_all x3 -> x0, starting transfers between devices: 11.1 us -> none  [the longest x1 4.23 us: local(): lax.all_to_all(sectioned[1], 'uly', split_axis=2, concat_axis=1, tiled=True)]
    all_to_all x1 -> x0, blocking collectives: 7.56 us -> none  [regroup_back(): lax.all_to_all(attended_part, 'uly', split_axis=1, concat_axis=2, tiled=T...]
    all_to_all x3 -> x0, waiting for transfers between devices: 6.09 us -> none  [the longest x1 3.81 us: local(): lax.all_to_all(sectioned[2], 'uly', split_axis=2, concat_axis=1, tiled=True)]
    reshape x8 -> x0, local copies, waits for them, and re-layouts: 5.84 us -> none  [the longest x6 4.8 us: split_heads(): return array.reshape(1, tokens, ulysses, heads_local, HD)]
    unnamed x2 -> x1, local copies, waits for them, and re-layouts: 0.01 us -> 1.62 us
    dot_general x2 -> x0, matrix products: 0.98 us -> none  [the longest x1 0.54 us: absorb(): jnp.einsum('hqk,khd->qhd', probabilities, value_piece, preferred_element_...]
  transfers between devices with their start and end apart: 3 -> 0, of which waited for: 2 -> 0; matrix products, arithmetic and copies ran while one was open for 6% -> 0% of each run, Pallas kernels for 0% -> 0%
where the time goes in v1:
time: 29.2 us; the launch traced here: 29.1 us
  Pallas kernels  27.5 us (94%)
  local copies, waits for them, and re-layouts  1.62 us (6%)
    pallas_call x1, Pallas kernels, exchanged(): pl.pallas_call(functools.partial(exchange_kernel, blocks, ulys, rows, hea...  27.5 us
    unnamed x1, local copies, waits for them, and re-layouts  1.62 us

profile of v1, /device:TPU:0, one launch (start us, length us, event | category | flops | bytes accessed | tf_op | source)
XLA Modules:
  0.0 29.1 jit_solution(6404653686102317180)
XLA Ops:
  0.0 27.5 %shard_map.37 = bf16[1,64,1536]{2,1,0:T(8,128)(2,1)} custom-call(bf16[1,64,1536]{2,1,0:T(8,128)(2,1)} %q_ref.1, bf16[1,64,1536]{2,1,0:T(8,128)(2,1)} %k_ref.1, bf16[1,64,1536]{2,1,0:T(8,128)(2,1)} %v_ref.1), custom_call_target="tpu_custom_call" | custom-call | tf_op jit(solution)/shard_map/pallas_call | solution.py:266
  27.5 1.6 %copy.5 = bf16[1,64,1536]{2,1,0:T(8,128)(2,1)} copy(bf16[1,64,1536]{2,1,0:T(8,128)(2,1)} %shard_map.37) | data formatting | bytes 393216

commit v2 on v1

--- a/solution.py
+++ b/solution.py
@@ -86,7 +86,7 @@
 
 def exchange_kernel(
     blocks, ulys, rows, heads, q_ref, k_ref, v_ref, o_ref,
-    qb, kb, vb, pb, ob, in_send, in_recv, out_send, out_recv,
+    qb, kb, vb, pb, ob, in_send, in_recv, out_send, out_recv, row_in,
 ):
     peers = blocks * ulys
     column = heads // ulys
@@ -110,44 +110,74 @@
     def piece(t, head):
         return sources[t].at[0, :, pl.ds(head * HD, HD)]
 
-    def send_order(mz, mx):
-        half = blocks // 2
-        def rank(p):
-            pz, px = p // ulys, p % ulys
-            crosses = (pz < half) != (mz < half)
-            return (not crosses, -abs(pz - mz), px == mx)
-        return sorted((p for p in range(peers) if p != mz * ulys + mx), key=rank)
-
-    def copies(mp):
+    def half_of(pz):
+        return 2 * pz >= blocks
+
+    def copy_to(mp, s, t, p):
+        pz, px = p // ulys, p % ulys
+        return pltpu.make_async_remote_copy(
+            src_ref=piece(t, head_of(pz, px, s)),
+            dst_ref=buffers[t].at[s, pl.ds(mp * rows, rows)],
+            send_sem=in_send.at[s, t, p],
+            recv_sem=in_recv.at[s, t, mp],
+            device_id={"blk": pz, "uly": px},
+            device_id_type=MESH,
+        )
+
+    def later_order(mz, mx):
+        others = [p for p in range(peers) if p != mz * ulys + mx]
+        return sorted(
+            others,
+            key=lambda p: (half_of(p // ulys) == half_of(mz), abs(p // ulys - mz), p % ulys != mx),
+        )
+
+    def token(row, mz, mx, to):
+        pl.semaphore_signal(
+            row_in.at[row], inc=1, device_id={"blk": to, "uly": mx}, device_id_type=MESH
+        )
+
+    def send_inputs(mp):
         mz, mx = mp // ulys, mp % ulys
-        made = []
-        for s in range(slots):
+        inside = lambda pz: 0 <= pz < blocks
+
+        def early(targets):
+            for p in targets:
+                for t in range(3):
+                    copy_to(mp, 0, t, p).start()
+
+        sides = (mz - 1, mz + 1) if half_of(mz) else (mz + 1, mz - 1)
+        for pz in sides:
+            if inside(pz):
+                token(mz, mz, mx, pz)
+        early([pz * ulys + mx for pz in sides if inside(pz)])
+        early([mz * ulys + px for px in range(ulys) if px != mx])
+        for d in range(1, blocks):
+            for step in (mz - d, mz + d) if half_of(mz) else (mz + d, mz - d):
+                if not inside(step):
+                    continue
+                pl.semaphore_wait(row_in.at[step], 1)
+                onward = mz + 1 if step < mz else mz - 1
+                if inside(onward):
+                    token(step, mz, mx, onward)
+                early([step * ulys + px for px in range(ulys) if d > 1 or px != mx])
+        for s in range(1, slots):
             for group in ((0, 1), (2,)):
-                for p in send_order(mz, mx):
-                    pz, px = p // ulys, p % ulys
-                    if s >= counts[pz]:
-                        continue
-                    for t in group:
-                        made.append(
-                            pltpu.make_async_remote_copy(
-                                src_ref=piece(t, head_of(pz, px, s)),
-                                dst_ref=buffers[t].at[s, pl.ds(mp * rows, rows)],
-                                send_sem=in_send.at[s, t, p],
-                                recv_sem=in_recv.at[s, t, mp],
-                                device_id={"blk": pz, "uly": px},
-                                device_id_type=MESH,
-                            )
-                        )
-        return made
+                for p in later_order(mz, mx):
+                    if s < counts[p // ulys]:
+                        for t in group:
+                            copy_to(mp, s, t, p).start()
 
     barrier = pltpu.get_barrier_semaphore()
-    for d in range(1, peers):
-        peer = lax.rem(me + d, peers)
+
+    def greet(pz, px):
         pl.semaphore_signal(
-            barrier, inc=1,
-            device_id={"blk": peer // ulys, "uly": lax.rem(peer, ulys)},
-            device_id_type=MESH,
-        )
+            barrier, inc=1, device_id={"blk": pz, "uly": px}, device_id_type=MESH
+        )
+
+    pl.when(z > 0)(lambda: greet(z - 1, x))
+    pl.when(z < blocks - 1)(lambda: greet(z + 1, x))
+    for d in range(1, ulys):
+        greet(z, lax.rem(x + d, ulys))
     for mp in range(peers):
         @pl.when(me == mp)
         def _():
@@ -157,13 +187,13 @@
                         piece(t, head), buffers[t].at[s, pl.ds(mp * rows, rows)],
                         in_recv.at[s, t, mp],
                     ).start()
-    pl.semaphore_wait(barrier, peers - 1)
+    greeted = (ulys - 1) + jnp.where(z > 0, 1, 0) + jnp.where(z < blocks - 1, 1, 0)
+    pl.semaphore_wait(barrier, greeted)
 
     for mp in range(peers):
         @pl.when(me == mp)
         def _():
-            for copy in copies(mp):
-                copy.start()
+            send_inputs(mp)
 
     first = jnp.int32(0)
     for i in range(blocks):
@@ -247,8 +277,11 @@
         @pl.when(me == mp)
         def _():
             mz, mx = mp // ulys, mp % ulys
-            for copy in copies(mp):
-                copy.wait_send()
+            for p in range(peers):
+                for s in range(counts[p // ulys]):
+                    for t in range(3):
+                        if p != mp:
+                            copy_to(mp, s, t, p).wait_send()
             for s in range(counts[mz]):
                 for p in range(peers):
                     if p != mp:
@@ -265,9 +298,9 @@
     total = peers * rows
     return pl.pallas_call(
         functools.partial(exchange_kernel, blocks, ulys, rows, heads),
-        out_shape=jax.ShapeDtypeStruct(query_rows.shape, jnp.bfloat16),
+        out_shape=pltpu.VMEM(query_rows.shape, jnp.bfloat16),
         in_specs=[pl.BlockSpec(memory_space=pl.ANY)] * 3,
-        out_specs=pl.BlockSpec(memory_space=pl.ANY),
+        out_specs=pl.BlockSpec(memory_space=pltpu.VMEM),
         scratch_shapes=[
             pltpu.VMEM((slots, total, HD), jnp.bfloat16),
             pltpu.VMEM((slots, total, HD), jnp.bfloat16),
@@ -278,6 +311,7 @@
             pltpu.SemaphoreType.DMA((slots, 3, peers)),
             pltpu.SemaphoreType.DMA((slots, peers)),
             pltpu.SemaphoreType.DMA((heads,)),
+            pltpu.SemaphoreType.REGULAR((blocks,)),
         ],
         compiler_params=pltpu.CompilerParams(collective_id=0, has_side_effects=True),
     )(query_rows, key_rows, value_rows)

time: 29.2 us -> 27 us (0.925)
  Pallas kernels: 27.5 us -> 26.2 us
  local copies, waits for them, and re-layouts: 1.62 us -> 0.68 us
    pallas_call x1, Pallas kernels: 27.5 us -> 26.2 us  [exchanged(): pl.pallas_call(functools.partial(exchange_kernel, blocks, ulys, rows, hea...]
    unnamed x1, local copies, waits for them, and re-layouts: 1.62 us -> 0.68 us
where the time goes in v2:
time: 27 us; the launch traced here: 26.9 us
  Pallas kernels  26.2 us (97%)
  local copies, waits for them, and re-layouts  0.68 us (3%)
    pallas_call x1, Pallas kernels, exchanged(): pl.pallas_call(functools.partial(exchange_kernel, blocks, ulys, rows, hea...  26.2 us
    unnamed x1, local copies, waits for them, and re-layouts  0.68 us

profile of v2, /device:TPU:0, one launch (start us, length us, event | category | flops | bytes accessed | tf_op | source)
XLA Modules:
  0.0 26.9 jit_solution(12862730113880836114)
XLA Ops:
  0.0 26.2 %shard_map.37 = bf16[1,64,1536]{2,1,0:T(8,128)(2,1)S(1)} custom-call(bf16[1,64,1536]{2,1,0:T(8,128)(2,1)} %q_ref.1, bf16[1,64,1536]{2,1,0:T(8,128)(2,1)} %k_ref.1, bf16[1,64,1536]{2,1,0:T(8,128)(2,1)} %v_ref.1), custom_call_target="tpu_custom_call" | custom-call | tf_op jit(solution)/shard_map/pallas_call | solution.py:299
  26.2 0.7 %copy.5 = bf16[1,64,1536]{2,1,0:T(8,128)(2,1)} copy(bf16[1,64,1536]{2,1,0:T(8,128)(2,1)S(1)} %shard_map.37) | data formatting | bytes 393216

commit v3 on v2

--- a/solution.py
+++ b/solution.py
@@ -101,71 +101,89 @@
     fold = (1.0 / math.sqrt(HD)) * math.log2(math.e)
     chunk_rows = ulys * rows
 
-    def head_of(pz, px, s):
-        return px * column + starts[pz] + s
-
-    def owned(pz, px):
-        return [head_of(pz, px, s) for s in range(counts[pz])]
+    def first_of(pz):
+        first = jnp.int32(0)
+        for i in range(blocks):
+            first = first + jnp.where(pz > i, counts[i], 0)
+        return first
+
+    def holds_at(pz, s):
+        has = pz < 0
+        for i in range(blocks):
+            if counts[i] > s:
+                has = jnp.logical_or(has, pz == i)
+        return has
+
+    my_head = x * column + first_of(z)
+    my_rows = pl.ds(pl.multiple_of(me * rows, rows), rows)
+    turn = jnp.where(z < blocks // 2, blocks // 2, 0)
 
     def piece(t, head):
-        return sources[t].at[0, :, pl.ds(head * HD, HD)]
-
-    def half_of(pz):
-        return 2 * pz >= blocks
-
-    def copy_to(mp, s, t, p):
-        pz, px = p // ulys, p % ulys
+        return sources[t].at[0, :, pl.ds(pl.multiple_of(head * HD, HD), HD)]
+
+    def copy_to(s, t, pz, px):
         return pltpu.make_async_remote_copy(
-            src_ref=piece(t, head_of(pz, px, s)),
-            dst_ref=buffers[t].at[s, pl.ds(mp * rows, rows)],
-            send_sem=in_send.at[s, t, p],
-            recv_sem=in_recv.at[s, t, mp],
+            src_ref=piece(t, px * column + first_of(pz) + s),
+            dst_ref=buffers[t].at[s, my_rows],
+            send_sem=in_send.at[s, t, pz * ulys + px],
+            recv_sem=in_recv.at[s, t, me],
             device_id={"blk": pz, "uly": px},
             device_id_type=MESH,
         )
 
-    def later_order(mz, mx):
-        others = [p for p in range(peers) if p != mz * ulys + mx]
-        return sorted(
-            others,
-            key=lambda p: (half_of(p // ulys) == half_of(mz), abs(p // ulys - mz), p % ulys != mx),
-        )
-
-    def token(row, mz, mx, to):
+    def send(s, pz, px):
+        for t in range(3):
+            copy_to(s, t, pz, px).start()
+
+    def token(row, to):
         pl.semaphore_signal(
-            row_in.at[row], inc=1, device_id={"blk": to, "uly": mx}, device_id_type=MESH
-        )
-
-    def send_inputs(mp):
-        mz, mx = mp // ulys, mp % ulys
-        inside = lambda pz: 0 <= pz < blocks
-
-        def early(targets):
-            for p in targets:
-                for t in range(3):
-                    copy_to(mp, 0, t, p).start()
-
-        sides = (mz - 1, mz + 1) if half_of(mz) else (mz + 1, mz - 1)
-        for pz in sides:
-            if inside(pz):
-                token(mz, mz, mx, pz)
-        early([pz * ulys + mx for pz in sides if inside(pz)])
-        early([mz * ulys + px for px in range(ulys) if px != mx])
+            row_in.at[row], inc=1, device_id={"blk": to, "uly": x}, device_id_type=MESH
+        )
+
+    toward = jnp.where(z < blocks // 2, 1, -1)
+
+    def inside(pz):
+        return jnp.logical_and(pz >= 0, pz < blocks)
+
+    def send_inputs():
+        def adjacent(side):
+            pz = z + side
+
+            @pl.when(inside(pz))
+            def _():
+                token(z, pz)
+                send(0, pz, x)
+
+        adjacent(toward)
+        adjacent(-toward)
+        for d in range(1, ulys):
+            send(0, z, lax.rem(x + d, ulys))
+
+        def further(d, side):
+            pz = z + side * d
+            onward = z - side
+
+            @pl.when(inside(pz))
+            def _():
+                pl.semaphore_wait(row_in.at[pz], 1)
+                pl.when(inside(onward))(lambda: token(pz, onward))
+                for e in range(1, ulys):
+                    send(0, pz, lax.rem(x + e, ulys))
+                if d > 1:
+                    send(0, pz, x)
+
         for d in range(1, blocks):
-            for step in (mz - d, mz + d) if half_of(mz) else (mz + d, mz - d):
-                if not inside(step):
-                    continue
-                pl.semaphore_wait(row_in.at[step], 1)
-                onward = mz + 1 if step < mz else mz - 1
-                if inside(onward):
-                    token(step, mz, mx, onward)
-                early([step * ulys + px for px in range(ulys) if d > 1 or px != mx])
+            further(d, toward)
+            further(d, -toward)
         for s in range(1, slots):
-            for group in ((0, 1), (2,)):
-                for p in later_order(mz, mx):
-                    if s < counts[p // ulys]:
-                        for t in group:
-                            copy_to(mp, s, t, p).start()
+            for i in range(blocks):
+                pz = lax.rem(turn + i, blocks)
+                for e in range(ulys):
+                    px = lax.rem(x + e, ulys)
+                    other = jnp.logical_or(pz != z, px != x)
+                    pl.when(jnp.logical_and(holds_at(pz, s), other))(
+                        functools.partial(send, s, pz, px)
+                    )
 
     barrier = pltpu.get_barrier_semaphore()
 
@@ -178,33 +196,26 @@
     pl.when(z < blocks - 1)(lambda: greet(z + 1, x))
     for d in range(1, ulys):
         greet(z, lax.rem(x + d, ulys))
-    for mp in range(peers):
-        @pl.when(me == mp)
-        def _():
-            for s, head in enumerate(owned(mp // ulys, mp % ulys)):
-                for t in range(3):
-                    pltpu.make_async_copy(
-                        piece(t, head), buffers[t].at[s, pl.ds(mp * rows, rows)],
-                        in_recv.at[s, t, mp],
-                    ).start()
+    def own(s):
+        for t in range(3):
+            pltpu.make_async_copy(
+                piece(t, my_head + s), buffers[t].at[s, my_rows], in_recv.at[s, t, me]
+            ).start()
+
+    for s in range(slots):
+        pl.when(holds_at(z, s))(functools.partial(own, s))
     greeted = (ulys - 1) + jnp.where(z > 0, 1, 0) + jnp.where(z < blocks - 1, 1, 0)
     pl.semaphore_wait(barrier, greeted)
 
-    for mp in range(peers):
-        @pl.when(me == mp)
-        def _():
-            send_inputs(mp)
-
-    first = jnp.int32(0)
-    for i in range(blocks):
-        first = first + jnp.where(z > i, counts[i], 0)
-    my_head = x * column + first
-    turn = jnp.where(z < blocks // 2, blocks // 2, 0)
+    send_inputs()
 
     def landed(s, t):
-        for p in range(peers):
-            block = buffers[t].at[s, pl.ds(p * rows, rows)]
+        def one(p, carry):
+            block = buffers[t].at[s, pl.ds(pl.multiple_of(p * rows, rows), rows)]
             pltpu.make_async_copy(block, block, in_recv.at[s, t, p]).wait()
+            return carry
+
+        lax.fori_loop(0, peers, one, 0)
 
     def out_copy(s, c, px):
         head = pl.multiple_of((my_head + s) * HD, HD)
@@ -224,12 +235,31 @@
         src, dst = out_copy(s, c, px)
         return pltpu.make_async_copy(src, dst, out_recv.at[my_head + s])
 
+    late = jnp.logical_and(lax.axis_index("cfg") == 1, holds_at(z, slots - 1))
+
+    def send_output(s, c):
+        for px in range(ulys):
+            mine = jnp.logical_and(c == z, x == px)
+
+            @pl.when(mine)
+            def _():
+                out_local(s, c, px).start()
+
+            @pl.when(jnp.logical_not(mine))
+            def _():
+                out_remote(s, c, px).start()
+
+    def send_late():
+        for s in range(slots - 1):
+            for i in range((blocks + 1) // 2):
+                send_output(s, jnp.where(z < blocks // 2, blocks - 1 - i, i))
+
     def one_slot(s):
         landed(s, 0)
         landed(s, 1)
         totals = []
         for i in range(blocks):
-            c = lax.rem(turn + i, blocks)
+            c = jnp.where(z < blocks // 2, blocks - 1 - i, i)
             span = pl.ds(pl.multiple_of(c * chunk_rows, chunk_rows), chunk_rows)
             scores = lax.dot_general(
                 qb[s, span, :], kb[s], (((1,), (1,)), ((), ())),
@@ -240,52 +270,44 @@
             totals.append(jnp.sum(weights, axis=1, keepdims=True))
             pb[span, :] = weights.astype(jnp.bfloat16)
         landed(s, 2)
+        if s > 0 and s == slots - 1:
+            pl.when(late)(send_late)
         for i in range(blocks):
-            c = lax.rem(turn + i, blocks)
+            c = jnp.where(z < blocks // 2, blocks - 1 - i, i)
             span = pl.ds(pl.multiple_of(c * chunk_rows, chunk_rows), chunk_rows)
             mixed = jnp.dot(pb[span, :], vb[s], preferred_element_type=jnp.float32)
             ob[s, span, :] = (mixed / totals[i]).astype(jnp.bfloat16)
-            for px in range(ulys):
-                mine = jnp.logical_and(c == z, x == px)
-
-                @pl.when(mine)
-                def _():
-                    out_local(s, c, px).start()
-
-                @pl.when(jnp.logical_not(mine))
-                def _():
-                    out_remote(s, c, px).start()
-
-    def holds(s):
-        has = z < 0
-        for i in range(blocks):
-            if counts[i] > s:
-                has = jnp.logical_or(has, z == i)
-        return has
+            if s < slots - 1 and 2 * i < blocks:
+                pl.when(jnp.logical_not(late))(functools.partial(send_output, s, c))
+            else:
+                send_output(s, c)
 
     for s in range(slots):
         if min(counts) > s:
             one_slot(s)
         else:
-            pl.when(holds(s))(functools.partial(one_slot, s))
-
-    for head in range(heads):
-        block = o_ref.at[0, :, pl.ds(head * HD, HD)]
+            pl.when(holds_at(z, s))(functools.partial(one_slot, s))
+
+    def result_landed(head, carry):
+        block = o_ref.at[0, :, pl.ds(pl.multiple_of(head * HD, HD), HD)]
         pltpu.make_async_copy(block, block, out_recv.at[head]).wait()
-
-    for mp in range(peers):
-        @pl.when(me == mp)
-        def _():
-            mz, mx = mp // ulys, mp % ulys
-            for p in range(peers):
-                for s in range(counts[p // ulys]):
-                    for t in range(3):
-                        if p != mp:
-                            copy_to(mp, s, t, p).wait_send()
-            for s in range(counts[mz]):
-                for p in range(peers):
-                    if p != mp:
-                        out_remote(s, p // ulys, p % ulys).wait_send()
+        return carry
+
+    def all_sent(p, carry):
+        pz, px = p // ulys, lax.rem(p, ulys)
+        for s in range(slots):
+            @pl.when(jnp.logical_and(p != me, holds_at(pz, s)))
+            def _():
+                for t in range(3):
+                    copy_to(s, t, pz, px).wait_send()
+
+            @pl.when(jnp.logical_and(p != me, holds_at(z, s)))
+            def _():
+                out_remote(s, pz, px).wait_send()
+        return carry
+
+    lax.fori_loop(0, peers, all_sent, 0)
+    lax.fori_loop(0, heads, result_landed, 0)
 
 
 def exchanged(query_rows, key_rows, value_rows):

time: 27 us -> 26.2 us (0.970)
  Pallas kernels: 26.2 us -> 25.4 us
    pallas_call x1, Pallas kernels: 26.2 us -> 25.4 us  [exchanged(): pl.pallas_call(functools.partial(exchange_kernel, blocks, ulys, rows, hea...]
where the time goes in v3:
time: 26.2 us; the launch traced here: 26 us
  Pallas kernels  25.4 us (97%)
  local copies, waits for them, and re-layouts  0.68 us (3%)
    pallas_call x1, Pallas kernels, exchanged(): pl.pallas_call(functools.partial(exchange_kernel, blocks, ulys, rows, hea...  25.4 us
    unnamed x1, local copies, waits for them, and re-layouts  0.68 us

profile of v3, /device:TPU:0, one launch (start us, length us, event | category | flops | bytes accessed | tf_op | source)
XLA Modules:
  0.0 26.0 jit_solution(12219629883547340419)
XLA Ops:
  0.0 25.4 %shard_map.37 = bf16[1,64,1536]{2,1,0:T(8,128)(2,1)S(1)} custom-call(bf16[1,64,1536]{2,1,0:T(8,128)(2,1)} %q_ref.1, bf16[1,64,1536]{2,1,0:T(8,128)(2,1)} %k_ref.1, bf16[1,64,1536]{2,1,0:T(8,128)(2,1)} %v_ref.1), custom_call_target="tpu_custom_call" | custom-call | tf_op jit(solution)/shard_map/pallas_call | solution.py:321
  25.4 0.7 %copy.5 = bf16[1,64,1536]{2,1,0:T(8,128)(2,1)} copy(bf16[1,64,1536]{2,1,0:T(8,128)(2,1)S(1)} %shard_map.37) | data formatting | bytes 393216

commit v4 on v3

--- a/solution.py
+++ b/solution.py
@@ -145,6 +145,8 @@
     def inside(pz):
         return jnp.logical_and(pz >= 0, pz < blocks)
 
+    paced = holds_at(z, slots - 1)
+
     def send_inputs():
         def adjacent(side):
             pz = z + side
@@ -175,6 +177,9 @@
         for d in range(1, blocks):
             further(d, toward)
             further(d, -toward)
+        pl.when(jnp.logical_not(paced))(send_rest)
+
+    def send_rest():
         for s in range(1, slots):
             for i in range(blocks):
                 pz = lax.rem(turn + i, blocks)
@@ -256,6 +261,8 @@
 
     def one_slot(s):
         landed(s, 0)
+        if s == 0:
+            pl.when(paced)(send_rest)
         landed(s, 1)
         totals = []
         for i in range(blocks):

time: 26.2 us -> 26.2 us (level)
  no operation moved by 1% of the time
where the time goes in v4:
time: 26.2 us; the launch traced here: 26 us
  Pallas kernels  25.4 us (97%)
  local copies, waits for them, and re-layouts  0.68 us (3%)
    pallas_call x1, Pallas kernels, exchanged(): pl.pallas_call(functools.partial(exchange_kernel, blocks, ulys, rows, hea...  25.4 us
    unnamed x1, local copies, waits for them, and re-layouts  0.68 us

profile of v4, /device:TPU:0, one launch (start us, length us, event | category | flops | bytes accessed | tf_op | source)
XLA Modules:
  0.0 26.0 jit_solution(13051661463162742390)
XLA Ops:
  0.0 25.4 %shard_map.37 = bf16[1,64,1536]{2,1,0:T(8,128)(2,1)S(1)} custom-call(bf16[1,64,1536]{2,1,0:T(8,128)(2,1)} %q_ref.1, bf16[1,64,1536]{2,1,0:T(8,128)(2,1)} %k_ref.1, bf16[1,64,1536]{2,1,0:T(8,128)(2,1)} %v_ref.1), custom_call_target="tpu_custom_call" | custom-call | tf_op jit(solution)/shard_map/pallas_call | solution.py:328
  25.4 0.7 %copy.5 = bf16[1,64,1536]{2,1,0:T(8,128)(2,1)} copy(bf16[1,64,1536]{2,1,0:T(8,128)(2,1)S(1)} %shard_map.37) | data formatting | bytes 393216
